TPU v7x, 256 devices: a whole 4x4x8 slice. The times are simulated.
256 devices in a mesh: dp: 16 (over z_hi, y), ctx: 16 (over x, z_lo, core).
Axes of the slice: x: 4, y: 4, z: 8 (z_hi: 4, z_lo: 2; z = z_hi * 2 + z_lo), core: 2. Of those that a mesh axis runs over, the one named last changes fastest.
Arguments:
- layer_input: bfloat16 [16, 2048, 4096], P('dp', 'ctx'), may hold values from -6 to 6
- query_states: bfloat16 [16, 2048, 512], P('dp', 'ctx'), may hold values from -9 to 9
- key_states: bfloat16 [16, 2048, 128], P('dp', 'ctx'), may hold values from -9 to 9
- value_states: bfloat16 [16, 2048, 128], P('dp', 'ctx'), may hold values from -6 to 6
- output_grad: bfloat16 [16, 2048, 512], P('dp', 'ctx'), may hold values from -6 to 6
- doc_lengths: int32 [16, 8], P('dp'), may hold values from 1 to 1024, 2048 in all within a row
Outputs:
- query_grad: bfloat16 [16, 2048, 512], P('dp', 'ctx')
- key_grad: bfloat16 [16, 2048, 128], P('dp', 'ctx')
- value_grad: bfloat16 [16, 2048, 128], P('dp', 'ctx')
- kv_weight_grad: float32 [4096, 256], P(('dp', 'ctx'))
All inputs are finite; a program needn't handle non-finite values.
Results may differ from a plain program's by a relative error of at most 0.014.
Values may be sent and summed in bfloat16 or wider, within the bound.
No kernel may reach another device: no remote copies, remote signals or barrier semaphores. Data moves between devices by JAX's collectives and lax.ppermute only.
A program may use at most 64 MiB of HBM per device.

v0:
```python
import math

import jax
import jax.numpy as jnp
from jax import lax
from jax.experimental import pallas as pl
from jax.experimental.pallas import tpu as pltpu
from jax.sharding import PartitionSpec as P


ROPE_BASE = 500000.0
NEG = -1e30
MIB = 1024 * 1024
B = 128
HEADS = 4
HALF = HEADS * 2 * B
NT = (((1,), (1,)), ((), ()))
TN = (((0,), (0,)), ((), ()))
NN = (((1,), (0,)), ((), ()))
SCALE = B**-0.5
LOG2E = 1.4426950408889634


VMEM = pl.BlockSpec(memory_space=pltpu.VMEM)
SMEM = pl.BlockSpec(memory_space=pltpu.SMEM)
HBM = pl.BlockSpec(memory_space=pltpu.HBM)


def dot(a, b, dims):
    return lax.dot_general(a, b, dims, preferred_element_type=jnp.float32)


def shape(dims, dtype):
    return jax.ShapeDtypeStruct(dims, dtype)


def rope_table(first):
    half = B // 2
    index = lax.broadcasted_iota(jnp.int32, (1, half), 1).astype(jnp.float32)
    frequency = jnp.exp(index * (-2.0 * math.log(ROPE_BASE) / B))
    position = first + lax.broadcasted_iota(jnp.int32, (B, 1), 0)
    angles = position.astype(jnp.float32) * frequency
    return jnp.concatenate([jnp.cos(angles), jnp.sin(angles)], 1)


def split_table(table):
    lane = lax.broadcasted_iota(jnp.int32, table.shape, 1)
    swapped = pltpu.roll(table, B // 2, 1)
    low = lane < B // 2
    return jnp.where(low, table, swapped), jnp.where(low, -swapped, table)


def rotated(u, cosine, sine):
    return u * cosine + pltpu.roll(u, B // 2, 1) * sine


def rows(index, size=B):
    return pl.ds(pl.multiple_of(index * size, size), size)


def prepare_kernel(
    where_ref, key_ref, value_ref, query_ref, grad_ref, x_ref, len_ref,
    kv_ref, qg_ref, q_out, x_out, len_out,
    key_s, query_s, sem,
):
    copies = [
        pltpu.make_async_copy(key_ref, key_s, sem.at[0]),
        pltpu.make_async_copy(query_ref, query_s, sem.at[1]),
        pltpu.make_async_copy(value_ref, kv_ref.at[:, B:], sem.at[2]),
        pltpu.make_async_copy(grad_ref, qg_ref.at[:, HEADS * B :], sem.at[3]),
        pltpu.make_async_copy(len_ref, len_out, sem.at[4]),
        pltpu.make_async_copy(x_ref, x_out, sem.at[5]),
    ]
    for copy in copies:
        copy.start()
    cosine, sine = split_table(rope_table(where_ref[0] * B))
    copies[0].wait()
    kv_ref[:, :B] = rotated(key_s[...].astype(jnp.float32), cosine, sine).astype(jnp.bfloat16)
    copies[1].wait()
    for h in range(HEADS):
        part = slice(h * B, (h + 1) * B)
        u = query_s[:, part].astype(jnp.float32)
        turned = rotated(u, cosine, sine).astype(jnp.bfloat16)
        qg_ref[:, part] = turned
        q_out[:, part] = turned
    for copy in copies[2:]:
        copy.wait()


def prepare(rank, keys, values, queries, grads, x, lengths):
    hbm = [pltpu.with_memory_space_constraint(a, pltpu.HBM) for a in (keys, values, queries, grads, x, lengths)]
    keys, values, queries, grads, x, lengths = hbm
    return pl.pallas_call(
        prepare_kernel,
        out_shape=(
            shape((B, 2 * B), jnp.bfloat16),
            shape((B, 2 * HEADS * B), jnp.bfloat16),
            shape((B, HEADS * B), jnp.bfloat16),
            shape((B, 4096), jnp.bfloat16),
            shape((1, 8), jnp.int32),
        ),
        in_specs=[SMEM] + [HBM] * 6,
        out_specs=(VMEM,) * 5,
        scratch_shapes=[
            pltpu.VMEM((B, B), jnp.bfloat16),
            pltpu.VMEM((B, HEADS * B), jnp.bfloat16),
            pltpu.SemaphoreType.DMA((6,)),
        ],
        compiler_params=pltpu.CompilerParams(vmem_limit_bytes=4 * MIB),
        name="prepare",
    )(rank, keys, values, queries, grads, x, lengths)


def slices_kernel(where_ref, x_ref, o0, o1, o2, o3, turned):
    slab = where_ref[0] // 4
    for i in range(32):
        tile = x_ref[:, i * B : (i + 1) * B].T
        for j in range(8):
            to, z, core = i % 2 * 2 + j // 4, j // 2 % 2, j % 2
            at = ((to * 2 + core) * 32 + i // 2 * 2 + z) * 16
            turned[at : at + 16, :] = tile[j * 16 : (j + 1) * 16, :]
    for k, out in enumerate((o0, o1, o2, o3)):
        out[...] = turned[rows((slab + k) % 4, 1024), :]


def slices(rank, x):
    return pl.pallas_call(
        slices_kernel,
        out_shape=[shape((1024, B), jnp.bfloat16)] * 4,
        in_specs=[SMEM, VMEM],
        out_specs=[VMEM] * 4,
        scratch_shapes=[pltpu.VMEM((4096, B), jnp.bfloat16)],
        compiler_params=pltpu.CompilerParams(vmem_limit_bytes=8 * MIB),
        cost_estimate=pl.CostEstimate(flops=0, bytes_accessed=2_000_000, transcendentals=0),
        name="slices",
    )(rank, x)


def tables_kernel(where_ref, tab_ref):
    rank = where_ref[0]
    for k in range(4):
        cosine, sine = split_table(rope_table(((rank // 4 - k + 4) % 4 * 4 + rank % 4) * B))
        tab_ref[k * B : (k + 1) * B, :B] = cosine
        tab_ref[k * B : (k + 1) * B, B:] = sine


def tables(rank):
    return pl.pallas_call(
        tables_kernel,
        out_shape=shape((4 * B, 2 * B), jnp.float32),
        in_specs=[SMEM],
        out_specs=VMEM,
        compiler_params=pltpu.CompilerParams(vmem_limit_bytes=4 * MIB),
        cost_estimate=pl.CostEstimate(flops=2_000_000, bytes_accessed=260_000, transcendentals=64_000),
        name="tables",
    )(rank)


def document_start(len_ref, position):
    start = position * 0
    end = jnp.int32(0)
    for d in range(8):
        end = end + len_ref[0, d]
        start = jnp.where(position >= end, end, start)
    return start


def column_keys(kvs):
    return jnp.concatenate([kv[:, :B] for kv in kvs], 0)


def heads_below(ref, first):
    return jnp.concatenate([ref[:, (first + h) * B : (first + h + 1) * B] for h in range(HEADS)], 0)


def by_source(qg0, qg1, q2, g2, q3, g3):
    for ref in (qg0, qg1):
        yield heads_below(ref, 0), heads_below(ref, HEADS)
    for q, g in ((q2, g2), (q3, g3)):
        yield heads_below(q, 0), heads_below(g, 0)


def in_lanes(rows_of_heads):
    return jnp.concatenate([rows_of_heads[h : h + 1, :] for h in range(HEADS)], 1)


def scores_kernel(
    where_ref, len_ref, kv0, kv1, kv2, qg0, qg1, q2, g2, q3, g3, p_ref, d_ref, stat_ref
):
    rank = where_ref[0]
    slab, col = rank // 4, rank % 4
    keys = column_keys((kv0, kv1, kv2))
    values = jnp.concatenate([kv[:, B:] for kv in (kv0, kv1, kv2)], 0)
    row = lax.broadcasted_iota(jnp.int32, (B, B), 0)
    for source, (queries, grads) in enumerate(by_source(qg0, qg1, q2, g2, q3, g3)):
        position = (slab * 4 + (col ^ source)) * B + lax.broadcasted_iota(jnp.int32, (1, B), 1)
        start = document_start(len_ref, position)
        allowed = jnp.concatenate(
            [
                (row >= start - (rank - 4 * b) * B) & (row <= position - rank * B)
                if b == 0
                else row >= start - (rank - 4 * b) * B
                for b in range(3)
            ],
            0,
        )
        for pair in range(2):
            part = slice(pair * 2 * B, (pair + 1) * 2 * B)
            s = dot(keys, queries[part], NT)
            d = dot(values, grads[part], NT)
            for h in range(2):
                here = slice(h * B, (h + 1) * B)
                lanes = slice((source * HEADS + pair * 2 + h) * B, (source * HEADS + pair * 2 + h + 1) * B)
                masked = jnp.where(allowed, s[:, here], NEG)
                top = jnp.max(masked, axis=0, keepdims=True)
                p = jnp.exp2((masked - top) * (SCALE * LOG2E))
                p_ref[:, lanes] = p
                d_ref[:, lanes] = d[:, here]
                sums = (top, jnp.sum(p, axis=0, keepdims=True), jnp.sum(p * d[:, here], axis=0, keepdims=True))
                for kind, value in enumerate(sums):
                    at = kind * 4 * HEADS + source * HEADS + pair * 2 + h
                    stat_ref[at : at + 1, :] = value


def scores(rank, lengths, kvs, qgs):
    wide = (3 * B, 2 * HALF)
    return pl.pallas_call(
        scores_kernel,
        out_shape=(
            shape(wide, jnp.float32),
            shape(wide, jnp.float32),
            shape((12 * HEADS, B), jnp.float32),
        ),
        in_specs=[SMEM, SMEM] + [VMEM] * 9,
        out_specs=(VMEM,) * 3,
        compiler_params=pltpu.CompilerParams(vmem_limit_bytes=20 * MIB),
        cost_estimate=pl.CostEstimate(flops=400_000_000, bytes_accessed=8_000_000, transcendentals=790_000),
        name="scores",
    )(rank, lengths, *kvs, *qgs)


def gradients_kernel(
    kv0, kv1, kv2, p_ref, d_ref, qg0, qg1, q2, g2, q3, g3, st0, st1, st2, st3,
    keep_ref, send_ref, dq0, dq1, dq2, dq3,
):
    keys = column_keys((kv0, kv1, kv2))
    dk = dv = None
    outs = (dq0, dq1, dq2, dq3)
    for source, (queries, grads) in enumerate(by_source(qg0, qg1, q2, g2, q3, g3)):
        tops, totals, sums = (
            [
                st[(kind * 4 + (source ^ bits)) * HEADS : (kind * 4 + (source ^ bits) + 1) * HEADS, :]
                for bits, st in enumerate((st0, st1, st2, st3))
            ]
            for kind in range(3)
        )
        top = jnp.maximum(jnp.maximum(tops[0], tops[1]), jnp.maximum(tops[2], tops[3]))
        factors = [jnp.exp2((t - top) * (SCALE * LOG2E)) for t in tops]
        inverse = 1.0 / sum(t * f for t, f in zip(totals, factors))
        delta = in_lanes(sum(t * f for t, f in zip(sums, factors)) * inverse)
        factor = in_lanes(factors[0] * inverse)
        lanes = slice(source * HEADS * B, (source + 1) * HEADS * B)
        p = p_ref[:, lanes] * factor
        ds = (p * (d_ref[:, lanes] - delta)).astype(jnp.bfloat16)
        more_v = dot(p.astype(jnp.bfloat16), grads, NN)
        more_k = dot(ds, queries, NN)
        dv = more_v if dv is None else dv + more_v
        dk = more_k if dk is None else dk + more_k
        outs[source][...] = dot(keys, ds, TN).astype(outs[source].dtype)
    dk = dk * SCALE
    keep_ref[:, :B] = dk
    keep_ref[:, B:] = dv
    send_ref[:, :B] = dk.astype(jnp.bfloat16)
    send_ref[:, B:] = dv.astype(jnp.bfloat16)


def gradients(kvs, p, d, qgs, stats):
    return pl.pallas_call(
        gradients_kernel,
        out_shape=(
            shape((3 * B, 2 * B), jnp.float32),
            shape((3 * B, 2 * B), jnp.bfloat16),
            shape((B, HEADS * B), jnp.float32),
            shape((B, HEADS * B), jnp.bfloat16),
            shape((B, HEADS * B), jnp.bfloat16),
            shape((B, HEADS * B), jnp.bfloat16),
        ),
        in_specs=[VMEM] * 15,
        out_specs=(VMEM,) * 6,
        compiler_params=pltpu.CompilerParams(vmem_limit_bytes=20 * MIB),
        cost_estimate=pl.CostEstimate(flops=600_000_000, bytes_accessed=8_000_000, transcendentals=8_000),
        name="gradients",
    )(*kvs, p, d, *qgs, *stats)


def query_end_kernel(mine_ref, r1, r2, r3, tab_ref, g01_ref, out_ref, key_ref, value_ref):
    key_ref[...] = g01_ref[:B, :B]
    value_ref[...] = g01_ref[:B, B:]
    cosine, sine = tab_ref[:B, :B], tab_ref[:B, B:]
    for h in range(HEADS):
        part = slice(h * B, (h + 1) * B)
        u = mine_ref[:, part]
        for ref in (r1, r2, r3):
            u = u + ref[:, part].astype(jnp.float32)
        out_ref[:, part] = rotated(u.T * SCALE, cosine, -sine).astype(jnp.bfloat16)


def query_end(mine, arrived, table, low):
    return pl.pallas_call(
        query_end_kernel,
        out_shape=(
            shape((B, HEADS * B), jnp.bfloat16),
            shape((B, B), jnp.bfloat16),
            shape((B, B), jnp.bfloat16),
        ),
        in_specs=[VMEM] * 6,
        out_specs=(VMEM,) * 3,
        compiler_params=pltpu.CompilerParams(vmem_limit_bytes=4 * MIB),
        cost_estimate=pl.CostEstimate(flops=300_000, bytes_accessed=900_000, transcendentals=0),
        name="query_end",
    )(mine, *arrived, table, low)


def weight_kernel(
    where_ref, keep_ref, r1, r2, r3, tab_ref, x0, x1, x2, x3,
    send_ref, g01_ref, g23_ref,
):
    core = where_ref[0] % 2

    def part(source, b, lanes):
        at = slice(b * B, (b + 1) * B)
        ref = (keep_ref, r1, r2, r3)[source]
        return ref[at, lanes * B : (lanes + 1) * B].astype(jnp.float32)

    grads = []
    for k in range(4):
        key, value = (
            part(k, 0, lanes) + part((k - 1) % 4, 1, lanes) + part((k - 2) % 4, 2, lanes) for lanes in (0, 1)
        )
        cosine, sine = tab_ref[k * B : (k + 1) * B, :B], tab_ref[k * B : (k + 1) * B, B:]
        key = rotated(key, cosine, -sine).astype(jnp.bfloat16)
        value = value.astype(jnp.bfloat16)
        grads.append(jnp.concatenate([key, value], 1))
    low, high = jnp.concatenate(grads[:2], 0), jnp.concatenate(grads[2:], 0)
    g01_ref[...] = low
    g23_ref[...] = high
    send_ref[...] = half_of_weight(1 - core, (x0, x1, x2, x3), low, high).astype(jnp.bfloat16)


def half_of_weight(core, xs, low, high):
    at = rows(core, 512)
    total = dot(jnp.concatenate([xs[0][at, :], xs[1][at, :]], 1), low, NN)
    return total + dot(jnp.concatenate([xs[2][at, :], xs[3][at, :]], 1), high, NN)


def own_half_kernel(where_ref, g01_ref, g23_ref, x0, x1, x2, x3, own_ref):
    core = where_ref[0] % 2
    own_ref[...] = half_of_weight(core, (x0, x1, x2, x3), g01_ref[...], g23_ref[...])


def own_half(rank, low, high, xs):
    return pl.pallas_call(
        own_half_kernel,
        out_shape=shape((512, 256), jnp.float32),
        in_specs=[SMEM] + [VMEM] * 6,
        out_specs=VMEM,
        compiler_params=pltpu.CompilerParams(vmem_limit_bytes=12 * MIB),
        cost_estimate=pl.CostEstimate(flops=134_000_000, bytes_accessed=1_800_000, transcendentals=0),
        name="own_half",
    )(rank, low, high, *xs)


def weight_part(rank, keep, arrived, table, xs):
    return pl.pallas_call(
        weight_kernel,
        out_shape=(
            shape((512, 256), jnp.bfloat16),
            shape((256, 256), jnp.bfloat16),
            shape((256, 256), jnp.bfloat16),
        ),
        in_specs=[SMEM] + [VMEM] * 9,
        out_specs=(VMEM,) * 3,
        compiler_params=pltpu.CompilerParams(vmem_limit_bytes=12 * MIB),
        cost_estimate=pl.CostEstimate(flops=134_000_000, bytes_accessed=3_000_000, transcendentals=0),
        name="weight",
    )(rank, keep, *arrived, table, *xs)


def weight_fold_kernel(own_ref, arrived_ref, out_ref, total, sem):
    copies = []
    for i in range(4):
        part = slice(i * B, (i + 1) * B)
        total[part, :] = (own_ref[part, :] + arrived_ref[part, :].astype(jnp.float32)).astype(jnp.bfloat16)
        copies.append(pltpu.make_async_copy(total.at[part], out_ref.at[part], sem.at[i]))
        copies[-1].start()
    for copy in copies:
        copy.wait()


def weight_fold(own, arrived):
    return pl.pallas_call(
        weight_fold_kernel,
        out_shape=shape((512, 256), jnp.bfloat16),
        in_specs=[VMEM, VMEM],
        out_specs=HBM,
        scratch_shapes=[pltpu.VMEM((512, 256), jnp.bfloat16), pltpu.SemaphoreType.DMA((4,))],
        compiler_params=pltpu.CompilerParams(vmem_limit_bytes=4 * MIB),
        cost_estimate=pl.CostEstimate(flops=131_072, bytes_accessed=1_000_000, transcendentals=0),
        name="weight_fold",
    )(own, arrived)


def compute(layer_input, query_states, key_states, value_states, output_grad, doc_lengths):
    where = lax.axis_index("ctx").astype(jnp.int32)[None]

    def permute(array, pairs):
        return lax.ppermute(array, "ctx", pairs)

    def around(array, slabs):
        return permute(array, [(i, (i + 4 * slabs) % 16) for i in range(16)])

    def swap(array, bits):
        return permute(array, [(i, i ^ bits) for i in range(16)])

    g_z = swap(output_grad[0], 2)
    kv, qg, q, x, lengths = prepare(
        where,
        key_states[0],
        value_states[0],
        query_states[0],
        output_grad[0],
        layer_input[0],
        doc_lengths,
    )
    q_z = swap(q, 2)
    kvs = [kv, around(kv, 1), around(kv, 2)]
    qg_c = swap(qg, 1)
    q_cz, g_cz = swap(q_z, 1), swap(g_z, 1)

    xs = slices(where, x)
    xs = [xs[0]] + [around(xs[k], k) for k in (1, 2, 3)]

    qgs = (qg, qg_c, q_z, g_z, q_cz, g_cz)
    p, d, stat = scores(where, lengths, kvs, qgs)
    stats = [stat] + [swap(stat, bits) for bits in (1, 2, 3)]
    table = tables(where)
    keep, send, mine, *others = gradients(kvs, p, d, qgs, stats)

    arrived = [around(send, k) for k in (1, 2, 3)]
    query_parts = [swap(part, bits) for bits, part in zip((1, 2, 3), others)]
    send, low, high = weight_part(where, keep, arrived, table, xs)
    arrived = swap(send, 1)
    own = own_half(where, low, high, xs)
    blocks = weight_fold(own, arrived).reshape(32, 16, 256)
    groups = [
        [dp * 16 + slab * 4 + z * 2 + core for dp in range(16) for z in range(2)]
        for slab in range(4)
        for core in range(2)
    ]
    blocks = lax.all_to_all(blocks, ("dp", "ctx"), split_axis=0, concat_axis=0, tiled=True, axis_index_groups=groups)
    query_grad, key_grad, value_grad = query_end(mine, query_parts, table, low)
    weight_grad = jnp.sum(blocks.astype(jnp.float32), axis=0)
    return query_grad[None], key_grad[None], value_grad[None], weight_grad


def solution(mesh):
    split = P("dp", "ctx", None)
    return jax.shard_map(
        compute,
        mesh=mesh,
        in_specs=(split,) * 5 + (P("dp", None),),
        out_specs=(split, split, split, P(("dp", "ctx"), None)),
        check_vma=False,
    )
```

profile of v0, /device:TPU:1, one launch (start us, length us, event | category | flops | bytes accessed | tf_op | source)
XLA Modules:
  0.0 79.3 jit_solution(6330735536965361275)
XLA Ops:
  0.6 1.5 %prepare.1 = (bf16[128,256]{1,0:T(8,128)(2,1)S(1)}, bf16[128,1024]{1,0:T(8,128)(2,1)S(1)}, bf16[128,512]{1,0:T(8,128)(2,1)S(1)}, bf16[128,4096]{1,0:T(8,128)(2,1)S(1)}, s32[1,8]{1,0:T(1,128)S(1)}) custom-call(s32[1]{0:T(128)} %bitcast.where_ref, bf16[128,128]{1,0:T(8,128)(2,1)} %bitcast.14, bf16[128,128]{1,0:T(8,128)(2,1)} %bitcast.15, ...), custom_call_target="tpu_custom_call" | custom-call | tf_op jit(solution)/shard_map/prepare/pallas_call | solution.py:93
  2.1 2.5 %collective-permute-start.3 = (bf16[128,512]{1,0:T(8,128)(2,1)S(1)}, bf16[128,512]{1,0:T(8,128)(2,1)S(1)}, u32[]{:S(2)}, u32[]{:S(2)}) collective-permute-start(bf16[128,512]{1,0:T(8,128)(2,1)S(1)} %get-tuple-element.31), channel_id=1, source_target_pairs={{0,2},{1,3},{2,0},{3,1},{4,6},{5,7},{6,4},{7,5},{8,10},{9,11},{10,... | collective-permute-start | bytes 393224 | tf_op jit(solution)/shard_map/ppermute | solution.py:417
  4.7 1.0 %collective-permute-start.2 = (bf16[128,1024]{1,0:T(8,128)(2,1)S(1)}, bf16[128,1024]{1,0:T(8,128)(2,1)S(1)}, u32[]{:S(2)}, u32[]{:S(2)}) collective-permute-start(bf16[128,1024]{1,0:T(8,128)(2,1)S(1)} %get-tuple-element.30.qg0), channel_id=1, source_target_pairs={{0,1},{1,0},{2,3},{3,2},{4,5},{5,4},{6,7},{7,6},{8,9},{9,8},{10,11... | collective-permute-start | bytes 786440 | tf_op jit(solution)/shard_map/ppermute | solution.py:417
  5.6 1.5 %collective-permute-start.4 = (bf16[128,512]{1,0:T(8,128)(2,1)}, bf16[128,512]{1,0:T(8,128)(2,1)S(1)}, u32[]{:S(2)}, u32[]{:S(2)}) collective-permute-start(bf16[128,512]{1,0:T(8,128)(2,1)} %bitcast.13), channel_id=1, source_target_pairs={{0,2},{1,3},{2,0},{3,1},{4,6},{5,7},{6,4},{7,5},{8,10},{9,11},{10,... | collective-permute-start | bytes 393224 | tf_op jit(solution)/shard_map/ppermute | solution.py:417
  7.2 0.4 slices.1
  7.6 0.1 collective-permute-start.16
  7.6 0.9 %collective-permute-start = (bf16[128,256]{1,0:T(8,128)(2,1)S(1)}, bf16[128,256]{1,0:T(8,128)(2,1)S(1)}, u32[]{:S(2)}, u32[]{:S(2)}) collective-permute-start(bf16[128,256]{1,0:T(8,128)(2,1)S(1)} %get-tuple-element.28.kv0), channel_id=1, source_target_pairs={{0,4},{1,5},{2,6},{3,7},{4,8},{5,9},{6,10},{7,11},{8,12},{9,13},{1... | collective-permute-start | bytes 196616 | tf_op jit(solution)/shard_map/ppermute | solution.py:417
  8.5 0.0 collective-permute-done.3.q2
  8.5 3.2 %collective-permute-start.5 = (bf16[128,512]{1,0:T(8,128)(2,1)S(1)}, bf16[128,512]{1,0:T(8,128)(2,1)S(1)}, u32[]{:S(2)}, u32[]{:S(2)}) collective-permute-start(bf16[128,512]{1,0:T(8,128)(2,1)S(1)} %collective-permute-done.3.q2), channel_id=1, source_target_pairs={{0,1},{1,0},{2,3},{3,2},{4,5},{5,4},{6,7},{7,6},{8,9},{9,8},{10,11... | collective-permute-start | bytes 393224 | tf_op jit(solution)/shard_map/ppermute | solution.py:417
  11.7 0.0 collective-permute-done.4.g2
  11.7 1.4 %collective-permute-start.6 = (bf16[128,512]{1,0:T(8,128)(2,1)S(1)}, bf16[128,512]{1,0:T(8,128)(2,1)S(1)}, u32[]{:S(2)}, u32[]{:S(2)}) collective-permute-start(bf16[128,512]{1,0:T(8,128)(2,1)S(1)} %collective-permute-done.4.g2), channel_id=1, source_target_pairs={{0,1},{1,0},{2,3},{3,2},{4,5},{5,4},{6,7},{7,6},{8,9},{9,8},{10,11... | collective-permute-start | bytes 393224 | tf_op jit(solution)/shard_map/ppermute | solution.py:417
  13.2 4.6 %collective-permute-done.kv1 = bf16[128,256]{1,0:T(8,128)(2,1)S(1)} collective-permute-done((bf16[128,256]{1,0:T(8,128)(2,1)S(1)}, bf16[128,256]{1,0:T(8,128)(2,1)S(1)}, u32[]{:S(2)}, u32[]{:S(2)}) %collective-permute-start) | collective-permute-done | bytes 65568 | tf_op jit(solution)/shard_map/ppermute | solution.py:417
  17.8 0.1 collective-permute-start.1
  17.9 4.5 %collective-permute-done.1.kv2 = bf16[128,256]{1,0:T(8,128)(2,1)S(1)} collective-permute-done((bf16[128,256]{1,0:T(8,128)(2,1)S(1)}, bf16[128,256]{1,0:T(8,128)(2,1)S(1)}, u32[]{:S(2)}, u32[]{:S(2)}) %collective-permute-start.1) | collective-permute-done | bytes 65568 | tf_op jit(solution)/shard_map/ppermute | solution.py:417
  22.4 0.0 collective-permute-done.5.q3
  22.4 0.0 collective-permute-done.2.qg1
  22.5 0.0 collective-permute-done.6.g3
  22.5 2.2 %scores.1 = (f32[384,2048]{1,0:T(8,128)S(1)}, f32[384,2048]{1,0:T(8,128)S(1)}, f32[48,128]{1,0:T(8,128)S(1)}) custom-call(s32[1]{0:T(128)} %bitcast.where_ref, s32[1,8]{1,0:T(1,128)S(1)} %get-tuple-element.29.len_ref, bf16[128,256]{1,0:T(8,128)(2,1)S(1)} %get-tuple-element.28.kv0, bf16[128,256]{1,0:T(8,128)(2,1)S(1)} %collective-permute-done.kv1, ...), custom_call_target="tpu_custom_call" | custom-call | flops 400000000 | bytes 8000000 | tf_op jit(solution)/shard_map/scores/pallas_call | solution.py:227
  24.6 2.4 %collective-permute-start.7 = (f32[48,128]{1,0:T(8,128)S(1)}, f32[48,128]{1,0:T(8,128)S(1)}, u32[]{:S(2)}, u32[]{:S(2)}) collective-permute-start(f32[48,128]{1,0:T(8,128)S(1)} %get-tuple-element.34.st0), channel_id=1, source_target_pairs={{0,1},{1,0},{2,3},{3,2},{4,5},{5,4},{6,7},{7,6},{8,9},{9,8},{10,11... | collective-permute-start | bytes 73736 | tf_op jit(solution)/shard_map/ppermute | solution.py:417
  27.0 0.0 collective-permute-start.8
  27.0 1.7 %collective-permute-start.9 = (f32[48,128]{1,0:T(8,128)S(1)}, f32[48,128]{1,0:T(8,128)S(1)}, u32[]{:S(2)}, u32[]{:S(2)}) collective-permute-start(f32[48,128]{1,0:T(8,128)S(1)} %get-tuple-element.34.st0), channel_id=1, source_target_pairs={{0,3},{1,2},{2,1},{3,0},{4,7},{5,6},{6,5},{7,4},{8,11},{9,10},{10,... | collective-permute-start | bytes 73736 | tf_op jit(solution)/shard_map/ppermute | solution.py:417
  28.8 0.0 collective-permute-start.17
  28.8 0.0 collective-permute-done.7.st1
  28.8 1.2 %collective-permute-start.18 = (bf16[1024,128]{1,0:T(8,128)(2,1)S(1)}, bf16[1024,128]{1,0:T(8,128)(2,1)S(1)}, u32[]{:S(2)}, u32[]{:S(2)}) collective-permute-start(bf16[1024,128]{1,0:T(8,128)(2,1)S(1)} %get-tuple-element.45), channel_id=1, source_target_pairs={{0,12},{1,13},{2,14},{3,15},{4,0},{5,1},{6,2},{7,3},{8,4},{9,5},{1... | collective-permute-start | bytes 786440 | tf_op jit(solution)/shard_map/ppermute | solution.py:417
  29.9 0.0 collective-permute-done.8.st2
  29.9 0.6 collective-permute-done.9.st3
  30.6 1.4 %gradients.1 = (f32[384,256]{1,0:T(8,128)S(1)}, bf16[384,256]{1,0:T(8,128)(2,1)S(1)}, f32[128,512]{1,0:T(8,128)S(1)}, bf16[128,512]{1,0:T(8,128)(2,1)S(1)}, bf16...) custom-call(bf16[128,256]{1,0:T(8,128)(2,1)S(1)} %get-tuple-element.28.kv0, ...), custom_call_target="tpu_custom_call" | custom-call | flops 600000000 | bytes 8000000 | tf_op jit(solution)/shard_map/gradients/pallas_call | solution.py:278
  31.9 0.1 collective-permute-start.13
  32.0 2.6 %collective-permute-start.14 = (bf16[384,256]{1,0:T(8,128)(2,1)S(1)}, bf16[384,256]{1,0:T(8,128)(2,1)S(1)}, u32[]{:S(2)}, u32[]{:S(2)}) collective-permute-start(bf16[384,256]{1,0:T(8,128)(2,1)S(1)} %get-tuple-element.40), channel_id=1, source_target_pairs={{0,8},{1,9},{2,10},{3,11},{4,12},{5,13},{6,14},{7,15},{8,0},{9,1},... | collective-permute-start | bytes 589832 | tf_op jit(solution)/shard_map/ppermute | solution.py:417
  34.6 0.0 collective-permute-done.16.x1
  34.6 0.6 collective-permute-start.15
  35.3 1.1 %tables.1.tab_ref = f32[512,256]{1,0:T(8,128)S(1)} custom-call(s32[1]{0:T(128)} %bitcast.where_ref), custom_call_target="tpu_custom_call" | custom-call | flops 2000000 | bytes 260000 | tf_op jit(solution)/shard_map/tables/pallas_call | solution.py:148
  36.4 1.7 %collective-permute-done.17.x2 = bf16[1024,128]{1,0:T(8,128)(2,1)S(1)} collective-permute-done((bf16[1024,128]{1,0:T(8,128)(2,1)S(1)}, bf16[1024,128]{1,0:T(8,128)(2,1)S(1)}, u32[]{:S(2)}, u32[]{:S(2)}) %collective-permute-start.17) | collective-permute-done | bytes 262176 | tf_op jit(solution)/shard_map/ppermute | solution.py:417
  38.0 3.0 %collective-permute-done.18.x3 = bf16[1024,128]{1,0:T(8,128)(2,1)S(1)} collective-permute-done((bf16[1024,128]{1,0:T(8,128)(2,1)S(1)}, bf16[1024,128]{1,0:T(8,128)(2,1)S(1)}, u32[]{:S(2)}, u32[]{:S(2)}) %collective-permute-start.18) | collective-permute-done | bytes 262176 | tf_op jit(solution)/shard_map/ppermute | solution.py:417
  41.0 2.2 %collective-permute-done.13.r1 = bf16[384,256]{1,0:T(8,128)(2,1)S(1)} collective-permute-done((bf16[384,256]{1,0:T(8,128)(2,1)S(1)}, bf16[384,256]{1,0:T(8,128)(2,1)S(1)}, u32[]{:S(2)}, u32[]{:S(2)}) %collective-permute-start.13) | collective-permute-done | bytes 196640 | tf_op jit(solution)/shard_map/ppermute | solution.py:417
  43.2 3.3 %collective-permute-done.14.r2 = bf16[384,256]{1,0:T(8,128)(2,1)S(1)} collective-permute-done((bf16[384,256]{1,0:T(8,128)(2,1)S(1)}, bf16[384,256]{1,0:T(8,128)(2,1)S(1)}, u32[]{:S(2)}, u32[]{:S(2)}) %collective-permute-start.14) | collective-permute-done | bytes 196640 | tf_op jit(solution)/shard_map/ppermute | solution.py:417
  46.5 3.0 %collective-permute-done.15.r3 = bf16[384,256]{1,0:T(8,128)(2,1)S(1)} collective-permute-done((bf16[384,256]{1,0:T(8,128)(2,1)S(1)}, bf16[384,256]{1,0:T(8,128)(2,1)S(1)}, u32[]{:S(2)}, u32[]{:S(2)}) %collective-permute-start.15) | collective-permute-done | bytes 196640 | tf_op jit(solution)/shard_map/ppermute | solution.py:417
  49.5 0.4 weight.1
  49.9 1.1 %collective-permute-start.19 = (bf16[512,256]{1,0:T(8,128)(2,1)S(1)}, bf16[512,256]{1,0:T(8,128)(2,1)S(1)}, u32[]{:S(2)}, u32[]{:S(2)}) collective-permute-start(bf16[512,256]{1,0:T(8,128)(2,1)S(1)} %get-tuple-element.51), channel_id=1, source_target_pairs={{0,1},{1,0},{2,3},{3,2},{4,5},{5,4},{6,7},{7,6},{8,9},{9,8},{10,11... | collective-permute-start | bytes 786440 | tf_op jit(solution)/shard_map/ppermute | solution.py:417
  51.0 0.3 own_half.1.own_ref
  51.3 0.9 %collective-permute-done.19.arrived_ref = bf16[512,256]{1,0:T(8,128)(2,1)S(1)} collective-permute-done((bf16[512,256]{1,0:T(8,128)(2,1)S(1)}, bf16[512,256]{1,0:T(8,128)(2,1)S(1)}, u32[]{:S(2)}, u32[]{:S(2)}) %collective-permute-start.19) | collective-permute-done | bytes 262176 | tf_op jit(solution)/shard_map/ppermute | solution.py:417
  52.1 0.7 weight_fold.1
  52.9 11.0 %all-to-all-start = ((bf16[32,16,256]{2,1,0:T(8,128)(2,1)}), bf16[32,16,256]{2,1,0:T(8,128)(2,1)S(1)}, u32[]{:S(2)}, u32[]{:S(2)}) async-start(bf16[32,16,256]{2,1,0:T(8,128)(2,1)} %bitcast.9), calls=%async_computation | async-start | bytes 524288 | tf_op jit(solution)/shard_map/all_to_all | solution.py:460
  64.0 0.7 collective-permute-start.10
  64.7 1.5 %collective-permute-start.11 = (bf16[128,512]{1,0:T(8,128)(2,1)S(1)}, bf16[128,512]{1,0:T(8,128)(2,1)S(1)}, u32[]{:S(2)}, u32[]{:S(2)}) collective-permute-start(bf16[128,512]{1,0:T(8,128)(2,1)S(1)} %get-tuple-element.37), channel_id=1, source_target_pairs={{0,2},{1,3},{2,0},{3,1},{4,6},{5,7},{6,4},{7,5},{8,10},{9,11},{10,... | collective-permute-start | bytes 393224 | tf_op jit(solution)/shard_map/ppermute | solution.py:417
  66.2 0.2 collective-permute-start.12
  66.4 0.0 collective-permute-done.10.r1
  66.4 7.3 %collective-permute-done.11.r2 = bf16[128,512]{1,0:T(8,128)(2,1)S(1)} collective-permute-done((bf16[128,512]{1,0:T(8,128)(2,1)S(1)}, bf16[128,512]{1,0:T(8,128)(2,1)S(1)}, u32[]{:S(2)}, u32[]{:S(2)}) %collective-permute-start.11) | collective-permute-done | bytes 131104 | tf_op jit(solution)/shard_map/ppermute | solution.py:417
  73.8 4.0 %collective-permute-done.12.r3 = bf16[128,512]{1,0:T(8,128)(2,1)S(1)} collective-permute-done((bf16[128,512]{1,0:T(8,128)(2,1)S(1)}, bf16[128,512]{1,0:T(8,128)(2,1)S(1)}, u32[]{:S(2)}, u32[]{:S(2)}) %collective-permute-start.12) | collective-permute-done | bytes 131104 | tf_op jit(solution)/shard_map/ppermute | solution.py:417
  77.8 0.9 %query_end.1 = (bf16[128,512]{1,0:T(8,128)(2,1)}, bf16[128,128]{1,0:T(8,128)(2,1)}, bf16[128,128]{1,0:T(8,128)(2,1)}) custom-call(f32[128,512]{1,0:T(8,128)S(1)} %get-tuple-element.35.mine_ref, bf16[128,512]{1,0:T(8,128)(2,1)S(1)} %collective-permute-done.10.r1, bf16[128,512]{1,0:T(8,128)(2,1)S(1)} %collective-permute-done.11.r2, ...), custom_call_target="tpu_custom_call" | custom-call | flops 300000 | bytes 900000 | tf_op jit(solution)/shard_map/query_end/pallas_call | solution.py:309
  78.7 0.0 all-to-all-done
  78.7 0.7 convert_reduce_fusion
Async XLA Ops:
  2.1 6.4 %collective-permute-start.3 = (bf16[128,512]{1,0:T(8,128)(2,1)S(1)}, bf16[128,512]{1,0:T(8,128)(2,1)S(1)}, u32[]{:S(2)}, u32[]{:S(2)}) collective-permute-start(bf16[128,512]{1,0:T(8,128)(2,1)S(1)} %get-tuple-element.31), channel_id=1, source_target_pairs={{0,2},{1,3},{2,0},{3,1},{4,6},{5,7},{6,4},{7,5},{8,10},{9,11},{10,... | collective-permute-start | bytes 393224 | tf_op jit(solution)/shard_map/ppermute | solution.py:417
  4.7 17.8 %collective-permute-start.2 = (bf16[128,1024]{1,0:T(8,128)(2,1)S(1)}, bf16[128,1024]{1,0:T(8,128)(2,1)S(1)}, u32[]{:S(2)}, u32[]{:S(2)}) collective-permute-start(bf16[128,1024]{1,0:T(8,128)(2,1)S(1)} %get-tuple-element.30.qg0), channel_id=1, source_target_pairs={{0,1},{1,0},{2,3},{3,2},{4,5},{5,4},{6,7},{7,6},{8,9},{9,8},{10,11... | collective-permute-start | bytes 786440 | tf_op jit(solution)/shard_map/ppermute | solution.py:417
  5.6 6.1 %collective-permute-start.4 = (bf16[128,512]{1,0:T(8,128)(2,1)}, bf16[128,512]{1,0:T(8,128)(2,1)S(1)}, u32[]{:S(2)}, u32[]{:S(2)}) collective-permute-start(bf16[128,512]{1,0:T(8,128)(2,1)} %bitcast.13), channel_id=1, source_target_pairs={{0,2},{1,3},{2,0},{3,1},{4,6},{5,7},{6,4},{7,5},{8,10},{9,11},{10,... | collective-permute-start | bytes 393224 | tf_op jit(solution)/shard_map/ppermute | solution.py:417
  7.6 27.1 %collective-permute-start.16 = (bf16[1024,128]{1,0:T(8,128)(2,1)S(1)}, bf16[1024,128]{1,0:T(8,128)(2,1)S(1)}, u32[]{:S(2)}, u32[]{:S(2)}) collective-permute-start(bf16[1024,128]{1,0:T(8,128)(2,1)S(1)} %get-tuple-element.43), channel_id=1, source_target_pairs={{0,4},{1,5},{2,6},{3,7},{4,8},{5,9},{6,10},{7,11},{8,12},{9,13},{1... | collective-permute-start | bytes 786440 | tf_op jit(solution)/shard_map/ppermute | solution.py:417
  7.6 10.2 %collective-permute-start = (bf16[128,256]{1,0:T(8,128)(2,1)S(1)}, bf16[128,256]{1,0:T(8,128)(2,1)S(1)}, u32[]{:S(2)}, u32[]{:S(2)}) collective-permute-start(bf16[128,256]{1,0:T(8,128)(2,1)S(1)} %get-tuple-element.28.kv0), channel_id=1, source_target_pairs={{0,4},{1,5},{2,6},{3,7},{4,8},{5,9},{6,10},{7,11},{8,12},{9,13},{1... | collective-permute-start | bytes 196616 | tf_op jit(solution)/shard_map/ppermute | solution.py:417
  8.5 13.9 %collective-permute-start.5 = (bf16[128,512]{1,0:T(8,128)(2,1)S(1)}, bf16[128,512]{1,0:T(8,128)(2,1)S(1)}, u32[]{:S(2)}, u32[]{:S(2)}) collective-permute-start(bf16[128,512]{1,0:T(8,128)(2,1)S(1)} %collective-permute-done.3.q2), channel_id=1, source_target_pairs={{0,1},{1,0},{2,3},{3,2},{4,5},{5,4},{6,7},{7,6},{8,9},{9,8},{10,11... | collective-permute-start | bytes 393224 | tf_op jit(solution)/shard_map/ppermute | solution.py:417
  11.7 10.7 %collective-permute-start.6 = (bf16[128,512]{1,0:T(8,128)(2,1)S(1)}, bf16[128,512]{1,0:T(8,128)(2,1)S(1)}, u32[]{:S(2)}, u32[]{:S(2)}) collective-permute-start(bf16[128,512]{1,0:T(8,128)(2,1)S(1)} %collective-permute-done.4.g2), channel_id=1, source_target_pairs={{0,1},{1,0},{2,3},{3,2},{4,5},{5,4},{6,7},{7,6},{8,9},{9,8},{10,11... | collective-permute-start | bytes 393224 | tf_op jit(solution)/shard_map/ppermute | solution.py:417
  17.8 4.6 %collective-permute-start.1 = (bf16[128,256]{1,0:T(8,128)(2,1)S(1)}, bf16[128,256]{1,0:T(8,128)(2,1)S(1)}, u32[]{:S(2)}, u32[]{:S(2)}) collective-permute-start(bf16[128,256]{1,0:T(8,128)(2,1)S(1)} %get-tuple-element.28.kv0), channel_id=1, source_target_pairs={{0,8},{1,9},{2,10},{3,11},{4,12},{5,13},{6,14},{7,15},{8,0},{9,1},... | collective-permute-start | bytes 196616 | tf_op jit(solution)/shard_map/ppermute | solution.py:417
  24.6 4.1 %collective-permute-start.7 = (f32[48,128]{1,0:T(8,128)S(1)}, f32[48,128]{1,0:T(8,128)S(1)}, u32[]{:S(2)}, u32[]{:S(2)}) collective-permute-start(f32[48,128]{1,0:T(8,128)S(1)} %get-tuple-element.34.st0), channel_id=1, source_target_pairs={{0,1},{1,0},{2,3},{3,2},{4,5},{5,4},{6,7},{7,6},{8,9},{9,8},{10,11... | collective-permute-start | bytes 73736 | tf_op jit(solution)/shard_map/ppermute | solution.py:417
  27.0 2.9 %collective-permute-start.8 = (f32[48,128]{1,0:T(8,128)S(1)}, f32[48,128]{1,0:T(8,128)S(1)}, u32[]{:S(2)}, u32[]{:S(2)}) collective-permute-start(f32[48,128]{1,0:T(8,128)S(1)} %get-tuple-element.34.st0), channel_id=1, source_target_pairs={{0,2},{1,3},{2,0},{3,1},{4,6},{5,7},{6,4},{7,5},{8,10},{9,11},{10,... | collective-permute-start | bytes 73736 | tf_op jit(solution)/shard_map/ppermute | solution.py:417
  27.0 3.5 %collective-permute-start.9 = (f32[48,128]{1,0:T(8,128)S(1)}, f32[48,128]{1,0:T(8,128)S(1)}, u32[]{:S(2)}, u32[]{:S(2)}) collective-permute-start(f32[48,128]{1,0:T(8,128)S(1)} %get-tuple-element.34.st0), channel_id=1, source_target_pairs={{0,3},{1,2},{2,1},{3,0},{4,7},{5,6},{6,5},{7,4},{8,11},{9,10},{10,... | collective-permute-start | bytes 73736 | tf_op jit(solution)/shard_map/ppermute | solution.py:417
  28.8 9.3 %collective-permute-start.17 = (bf16[1024,128]{1,0:T(8,128)(2,1)S(1)}, bf16[1024,128]{1,0:T(8,128)(2,1)S(1)}, u32[]{:S(2)}, u32[]{:S(2)}) collective-permute-start(bf16[1024,128]{1,0:T(8,128)(2,1)S(1)} %get-tuple-element.44), channel_id=1, source_target_pairs={{0,8},{1,9},{2,10},{3,11},{4,12},{5,13},{6,14},{7,15},{8,0},{9,1},... | collective-permute-start | bytes 786440 | tf_op jit(solution)/shard_map/ppermute | solution.py:417
  28.8 12.2 %collective-permute-start.18 = (bf16[1024,128]{1,0:T(8,128)(2,1)S(1)}, bf16[1024,128]{1,0:T(8,128)(2,1)S(1)}, u32[]{:S(2)}, u32[]{:S(2)}) collective-permute-start(bf16[1024,128]{1,0:T(8,128)(2,1)S(1)} %get-tuple-element.45), channel_id=1, source_target_pairs={{0,12},{1,13},{2,14},{3,15},{4,0},{5,1},{6,2},{7,3},{8,4},{9,5},{1... | collective-permute-start | bytes 786440 | tf_op jit(solution)/shard_map/ppermute | solution.py:417
  31.9 11.3 %collective-permute-start.13 = (bf16[384,256]{1,0:T(8,128)(2,1)S(1)}, bf16[384,256]{1,0:T(8,128)(2,1)S(1)}, u32[]{:S(2)}, u32[]{:S(2)}) collective-permute-start(bf16[384,256]{1,0:T(8,128)(2,1)S(1)} %get-tuple-element.40), channel_id=1, source_target_pairs={{0,4},{1,5},{2,6},{3,7},{4,8},{5,9},{6,10},{7,11},{8,12},{9,13},{1... | collective-permute-start | bytes 589832 | tf_op jit(solution)/shard_map/ppermute | solution.py:417
  32.0 14.5 %collective-permute-start.14 = (bf16[384,256]{1,0:T(8,128)(2,1)S(1)}, bf16[384,256]{1,0:T(8,128)(2,1)S(1)}, u32[]{:S(2)}, u32[]{:S(2)}) collective-permute-start(bf16[384,256]{1,0:T(8,128)(2,1)S(1)} %get-tuple-element.40), channel_id=1, source_target_pairs={{0,8},{1,9},{2,10},{3,11},{4,12},{5,13},{6,14},{7,15},{8,0},{9,1},... | collective-permute-start | bytes 589832 | tf_op jit(solution)/shard_map/ppermute | solution.py:417
  34.6 14.8 %collective-permute-start.15 = (bf16[384,256]{1,0:T(8,128)(2,1)S(1)}, bf16[384,256]{1,0:T(8,128)(2,1)S(1)}, u32[]{:S(2)}, u32[]{:S(2)}) collective-permute-start(bf16[384,256]{1,0:T(8,128)(2,1)S(1)} %get-tuple-element.40), channel_id=1, source_target_pairs={{0,12},{1,13},{2,14},{3,15},{4,0},{5,1},{6,2},{7,3},{8,4},{9,5},{1... | collective-permute-start | bytes 589832 | tf_op jit(solution)/shard_map/ppermute | solution.py:417
  49.9 2.2 %collective-permute-start.19 = (bf16[512,256]{1,0:T(8,128)(2,1)S(1)}, bf16[512,256]{1,0:T(8,128)(2,1)S(1)}, u32[]{:S(2)}, u32[]{:S(2)}) collective-permute-start(bf16[512,256]{1,0:T(8,128)(2,1)S(1)} %get-tuple-element.51), channel_id=1, source_target_pairs={{0,1},{1,0},{2,3},{3,2},{4,5},{5,4},{6,7},{7,6},{8,9},{9,8},{10,11... | collective-permute-start | bytes 786440 | tf_op jit(solution)/shard_map/ppermute | solution.py:417
  52.9 25.8 %all-to-all-start = ((bf16[32,16,256]{2,1,0:T(8,128)(2,1)}), bf16[32,16,256]{2,1,0:T(8,128)(2,1)S(1)}, u32[]{:S(2)}, u32[]{:S(2)}) async-start(bf16[32,16,256]{2,1,0:T(8,128)(2,1)} %bitcast.9), calls=%async_computation | async-start | bytes 524288 | tf_op jit(solution)/shard_map/all_to_all | solution.py:460
  64.0 2.5 %collective-permute-start.10 = (bf16[128,512]{1,0:T(8,128)(2,1)S(1)}, bf16[128,512]{1,0:T(8,128)(2,1)S(1)}, u32[]{:S(2)}, u32[]{:S(2)}) collective-permute-start(bf16[128,512]{1,0:T(8,128)(2,1)S(1)} %get-tuple-element.36), channel_id=1, source_target_pairs={{0,1},{1,0},{2,3},{3,2},{4,5},{5,4},{6,7},{7,6},{8,9},{9,8},{10,11... | collective-permute-start | bytes 393224 | tf_op jit(solution)/shard_map/ppermute | solution.py:417
  64.7 9.1 %collective-permute-start.11 = (bf16[128,512]{1,0:T(8,128)(2,1)S(1)}, bf16[128,512]{1,0:T(8,128)(2,1)S(1)}, u32[]{:S(2)}, u32[]{:S(2)}) collective-permute-start(bf16[128,512]{1,0:T(8,128)(2,1)S(1)} %get-tuple-element.37), channel_id=1, source_target_pairs={{0,2},{1,3},{2,0},{3,1},{4,6},{5,7},{6,4},{7,5},{8,10},{9,11},{10,... | collective-permute-start | bytes 393224 | tf_op jit(solution)/shard_map/ppermute | solution.py:417
  66.2 11.6 %collective-permute-start.12 = (bf16[128,512]{1,0:T(8,128)(2,1)S(1)}, bf16[128,512]{1,0:T(8,128)(2,1)S(1)}, u32[]{:S(2)}, u32[]{:S(2)}) collective-permute-start(bf16[128,512]{1,0:T(8,128)(2,1)S(1)} %get-tuple-element.38), channel_id=1, source_target_pairs={{0,3},{1,2},{2,1},{3,0},{4,7},{5,6},{6,5},{7,4},{8,11},{9,10},{10,... | collective-permute-start | bytes 393224 | tf_op jit(solution)/shard_map/ppermute | solution.py:417
where the time goes:
time: 79.5 us; the launch traced here: 79.3 us
  waiting for transfers between devices  35.1 us (44%)
  starting transfers between devices  34 us (43%)
  Pallas kernels  8.91 us (11%)
    ppermute x20, waiting for transfers between devices, permute(): return lax.ppermute(array, 'ctx', pairs)  35.1 us
    ppermute x20, starting transfers between devices, permute(): return lax.ppermute(array, 'ctx', pairs)  22.9 us
    all_to_all x1, starting transfers between devices, compute(): lax.all_to_all(blocks, ('dp', 'ctx'), split_axis=0, concat_axis=0, tiled=...  11 us
    pallas_call x1, Pallas kernels, scores(): pl.pallas_call(scores_kernel, out_shape=(shape(wide, jnp.float32), shape(...  2.18 us
  transfers between devices with their start and end apart: 21, of which 11 were waited for; matrix products, arithmetic and copies ran while one was open for 0% of the time, Pallas kernels for 8%

commit v1 on v0

--- a/solution.py
+++ b/solution.py
@@ -60,7 +60,7 @@
 
 def prepare_kernel(
     where_ref, key_ref, value_ref, query_ref, grad_ref, x_ref, len_ref,
-    kv_ref, qg_ref, q_out, x_out, len_out,
+    kv_ref, qg_ref, x_out, len_out,
     key_s, query_s, sem,
 ):
     copies = [
@@ -80,9 +80,7 @@
     for h in range(HEADS):
         part = slice(h * B, (h + 1) * B)
         u = query_s[:, part].astype(jnp.float32)
-        turned = rotated(u, cosine, sine).astype(jnp.bfloat16)
-        qg_ref[:, part] = turned
-        q_out[:, part] = turned
+        qg_ref[:, part] = rotated(u, cosine, sine).astype(jnp.bfloat16)
     for copy in copies[2:]:
         copy.wait()
 
@@ -95,12 +93,11 @@
         out_shape=(
             shape((B, 2 * B), jnp.bfloat16),
             shape((B, 2 * HEADS * B), jnp.bfloat16),
-            shape((B, HEADS * B), jnp.bfloat16),
             shape((B, 4096), jnp.bfloat16),
             shape((1, 8), jnp.int32),
         ),
         in_specs=[SMEM] + [HBM] * 6,
-        out_specs=(VMEM,) * 5,
+        out_specs=(VMEM,) * 4,
         scratch_shapes=[
             pltpu.VMEM((B, B), jnp.bfloat16),
             pltpu.VMEM((B, HEADS * B), jnp.bfloat16),
@@ -173,26 +170,19 @@
     return jnp.concatenate([ref[:, (first + h) * B : (first + h + 1) * B] for h in range(HEADS)], 0)
 
 
-def by_source(qg0, qg1, q2, g2, q3, g3):
-    for ref in (qg0, qg1):
-        yield heads_below(ref, 0), heads_below(ref, HEADS)
-    for q, g in ((q2, g2), (q3, g3)):
-        yield heads_below(q, 0), heads_below(g, 0)
-
-
 def in_lanes(rows_of_heads):
     return jnp.concatenate([rows_of_heads[h : h + 1, :] for h in range(HEADS)], 1)
 
 
 def scores_kernel(
-    where_ref, len_ref, kv0, kv1, kv2, qg0, qg1, q2, g2, q3, g3, p_ref, d_ref, stat_ref
+    where_ref, len_ref, kv0, kv1, kv2, qg0, qg1, qg2, qg3, p_ref, d_ref, stat_ref
 ):
     rank = where_ref[0]
     slab, col = rank // 4, rank % 4
     keys = column_keys((kv0, kv1, kv2))
     values = jnp.concatenate([kv[:, B:] for kv in (kv0, kv1, kv2)], 0)
     row = lax.broadcasted_iota(jnp.int32, (B, B), 0)
-    for source, (queries, grads) in enumerate(by_source(qg0, qg1, q2, g2, q3, g3)):
+    for source, ref in enumerate((qg0, qg1, qg2, qg3)):
         position = (slab * 4 + (col ^ source)) * B + lax.broadcasted_iota(jnp.int32, (1, B), 1)
         start = document_start(len_ref, position)
         allowed = jnp.concatenate(
@@ -204,6 +194,7 @@
             ],
             0,
         )
+        queries, grads = heads_below(ref, 0), heads_below(ref, HEADS)
         for pair in range(2):
             part = slice(pair * 2 * B, (pair + 1) * 2 * B)
             s = dot(keys, queries[part], NT)
@@ -231,7 +222,7 @@
             shape(wide, jnp.float32),
             shape((12 * HEADS, B), jnp.float32),
         ),
-        in_specs=[SMEM, SMEM] + [VMEM] * 9,
+        in_specs=[SMEM, SMEM] + [VMEM] * 7,
         out_specs=(VMEM,) * 3,
         compiler_params=pltpu.CompilerParams(vmem_limit_bytes=20 * MIB),
         cost_estimate=pl.CostEstimate(flops=400_000_000, bytes_accessed=8_000_000, transcendentals=790_000),
@@ -240,13 +231,12 @@
 
 
 def gradients_kernel(
-    kv0, kv1, kv2, p_ref, d_ref, qg0, qg1, q2, g2, q3, g3, st0, st1, st2, st3,
+    kv0, kv1, kv2, p_ref, d_ref, qg0, qg1, qg2, qg3, st0, st1, st2, st3,
     keep_ref, send_ref, dq0, dq1, dq2, dq3,
 ):
     keys = column_keys((kv0, kv1, kv2))
     dk = dv = None
-    outs = (dq0, dq1, dq2, dq3)
-    for source, (queries, grads) in enumerate(by_source(qg0, qg1, q2, g2, q3, g3)):
+    for source, (ref, out) in enumerate(zip((qg0, qg1, qg2, qg3), (dq0, dq1, dq2, dq3))):
         tops, totals, sums = (
             [
                 st[(kind * 4 + (source ^ bits)) * HEADS : (kind * 4 + (source ^ bits) + 1) * HEADS, :]
@@ -262,11 +252,11 @@
         lanes = slice(source * HEADS * B, (source + 1) * HEADS * B)
         p = p_ref[:, lanes] * factor
         ds = (p * (d_ref[:, lanes] - delta)).astype(jnp.bfloat16)
-        more_v = dot(p.astype(jnp.bfloat16), grads, NN)
-        more_k = dot(ds, queries, NN)
+        more_v = dot(p.astype(jnp.bfloat16), heads_below(ref, HEADS), NN)
+        more_k = dot(ds, heads_below(ref, 0), NN)
         dv = more_v if dv is None else dv + more_v
         dk = more_k if dk is None else dk + more_k
-        outs[source][...] = dot(keys, ds, TN).astype(outs[source].dtype)
+        out[...] = dot(keys, ds, TN).astype(out.dtype)
     dk = dk * SCALE
     keep_ref[:, :B] = dk
     keep_ref[:, B:] = dv
@@ -285,7 +275,7 @@
             shape((B, HEADS * B), jnp.bfloat16),
             shape((B, HEADS * B), jnp.bfloat16),
         ),
-        in_specs=[VMEM] * 15,
+        in_specs=[VMEM] * 13,
         out_specs=(VMEM,) * 6,
         compiler_params=pltpu.CompilerParams(vmem_limit_bytes=20 * MIB),
         cost_estimate=pl.CostEstimate(flops=600_000_000, bytes_accessed=8_000_000, transcendentals=8_000),
@@ -422,8 +412,7 @@
     def swap(array, bits):
         return permute(array, [(i, i ^ bits) for i in range(16)])
 
-    g_z = swap(output_grad[0], 2)
-    kv, qg, q, x, lengths = prepare(
+    kv, qg, x, lengths = prepare(
         where,
         key_states[0],
         value_states[0],
@@ -432,21 +421,22 @@
         layer_input[0],
         doc_lengths,
     )
-    q_z = swap(q, 2)
+    qg_z = swap(qg, 2)
     kvs = [kv, around(kv, 1), around(kv, 2)]
     qg_c = swap(qg, 1)
-    q_cz, g_cz = swap(q_z, 1), swap(g_z, 1)
+    qg_cz = swap(qg_z, 1)
 
     xs = slices(where, x)
     xs = [xs[0]] + [around(xs[k], k) for k in (1, 2, 3)]
 
-    qgs = (qg, qg_c, q_z, g_z, q_cz, g_cz)
+    qgs = (qg, qg_c, qg_z, qg_cz)
     p, d, stat = scores(where, lengths, kvs, qgs)
     stats = [stat] + [swap(stat, bits) for bits in (1, 2, 3)]
     table = tables(where)
     keep, send, mine, *others = gradients(kvs, p, d, qgs, stats)
 
     arrived = [around(send, k) for k in (1, 2, 3)]
+    *others, arrived[1] = lax.optimization_barrier((*others, arrived[1]))
     query_parts = [swap(part, bits) for bits, part in zip((1, 2, 3), others)]
     send, low, high = weight_part(where, keep, arrived, table, xs)
     arrived = swap(send, 1)

time: 79.5 us -> 81.1 us (1.020)
  waiting for transfers between devices: 35.1 us -> 38.9 us
  starting transfers between devices: 34 us -> 31.7 us
    ppermute x20 -> x18, waiting for transfers between devices: 35.1 us -> 38.9 us  [permute(): return lax.ppermute(array, 'ctx', pairs)]
    ppermute x20 -> x18, starting transfers between devices: 22.9 us -> 21.4 us  [permute(): return lax.ppermute(array, 'ctx', pairs)]
  transfers between devices with their start and end apart: 21 -> 19, of which waited for: 11 -> 12; matrix products, arithmetic and copies ran while one was open for 0% -> 0% of each run, Pallas kernels for 8% -> 3%
where the time goes in v1:
time: 81.1 us; the launch traced here: 81 us
  waiting for transfers between devices  38.9 us (48%)
  starting transfers between devices  31.7 us (39%)
  Pallas kernels  8.95 us (11%)
    ppermute x18, waiting for transfers between devices, permute(): return lax.ppermute(array, 'ctx', pairs)  38.9 us
    ppermute x18, starting transfers between devices, permute(): return lax.ppermute(array, 'ctx', pairs)  21.4 us
    all_to_all x1, starting transfers between devices, compute(): lax.all_to_all(blocks, ('dp', 'ctx'), split_axis=0, concat_axis=0, tiled=...  10.3 us
    pallas_call x1, Pallas kernels, scores(): pl.pallas_call(scores_kernel, out_shape=(shape(wide, jnp.float32), shape(...  2.21 us
  transfers between devices with their start and end apart: 19, of which 12 were waited for; matrix products, arithmetic and copies ran while one was open for 0% of the time, Pallas kernels for 3%

profile of v1, /device:TPU:1, one launch (start us, length us, event | category | flops | bytes accessed | tf_op | source)
XLA Modules:
  0.0 81.0 jit_solution(13725881954153874091)
XLA Ops:
  0.6 1.5 %prepare.1 = (bf16[128,256]{1,0:T(8,128)(2,1)S(1)}, bf16[128,1024]{1,0:T(8,128)(2,1)S(1)}, bf16[128,4096]{1,0:T(8,128)(2,1)S(1)}, s32[1,8]{1,0:T(1,128)S(1)}) custom-call(s32[1]{0:T(128)} %bitcast.where_ref, bf16[128,128]{1,0:T(8,128)(2,1)} %bitcast.13, bf16[128,128]{1,0:T(8,128)(2,1)} %bitcast.14, bf16[128,512]{1,0:T(8,128)(2,1)} %bitcast.11, ...), custom_call_target="tpu_custom_call" | custom-call | tf_op jit(solution)/shard_map/prepare/pallas_call | solution.py:91
  2.1 2.5 %collective-permute-start.3 = (bf16[128,1024]{1,0:T(8,128)(2,1)S(1)}, bf16[128,1024]{1,0:T(8,128)(2,1)S(1)}, u32[]{:S(2)}, u32[]{:S(2)}) collective-permute-start(bf16[128,1024]{1,0:T(8,128)(2,1)S(1)} %get-tuple-element.33.qg0), channel_id=1, source_target_pairs={{0,2},{1,3},{2,0},{3,1},{4,6},{5,7},{6,4},{7,5},{8,10},{9,11},{10,... | collective-permute-start | bytes 786440 | tf_op jit(solution)/shard_map/ppermute | solution.py:407
  4.7 1.0 %collective-permute-start.2 = (bf16[128,1024]{1,0:T(8,128)(2,1)S(1)}, bf16[128,1024]{1,0:T(8,128)(2,1)S(1)}, u32[]{:S(2)}, u32[]{:S(2)}) collective-permute-start(bf16[128,1024]{1,0:T(8,128)(2,1)S(1)} %get-tuple-element.33.qg0), channel_id=1, source_target_pairs={{0,1},{1,0},{2,3},{3,2},{4,5},{5,4},{6,7},{7,6},{8,9},{9,8},{10,11... | collective-permute-start | bytes 786440 | tf_op jit(solution)/shard_map/ppermute | solution.py:407
  5.6 4.0 %collective-permute-done.3.qg2 = bf16[128,1024]{1,0:T(8,128)(2,1)S(1)} collective-permute-done((bf16[128,1024]{1,0:T(8,128)(2,1)S(1)}, bf16[128,1024]{1,0:T(8,128)(2,1)S(1)}, u32[]{:S(2)}, u32[]{:S(2)}) %collective-permute-start.3) | collective-permute-done | bytes 262176 | tf_op jit(solution)/shard_map/ppermute | solution.py:407
  9.7 2.3 %collective-permute-start.4 = (bf16[128,1024]{1,0:T(8,128)(2,1)S(1)}, bf16[128,1024]{1,0:T(8,128)(2,1)S(1)}, u32[]{:S(2)}, u32[]{:S(2)}) collective-permute-start(bf16[128,1024]{1,0:T(8,128)(2,1)S(1)} %collective-permute-done.3.qg2), channel_id=1, source_target_pairs={{0,1},{1,0},{2,3},{3,2},{4,5},{5,4},{6,7},{7,6},{8,9},{9,8},{10,11... | collective-permute-start | bytes 786440 | tf_op jit(solution)/shard_map/ppermute | solution.py:407
  11.9 1.2 %collective-permute-start = (bf16[128,256]{1,0:T(8,128)(2,1)S(1)}, bf16[128,256]{1,0:T(8,128)(2,1)S(1)}, u32[]{:S(2)}, u32[]{:S(2)}) collective-permute-start(bf16[128,256]{1,0:T(8,128)(2,1)S(1)} %get-tuple-element.31.kv0), channel_id=1, source_target_pairs={{0,4},{1,5},{2,6},{3,7},{4,8},{5,9},{6,10},{7,11},{8,12},{9,13},{1... | collective-permute-start | bytes 196616 | tf_op jit(solution)/shard_map/ppermute | solution.py:407
  13.1 2.5 %collective-permute-start.1 = (bf16[128,256]{1,0:T(8,128)(2,1)S(1)}, bf16[128,256]{1,0:T(8,128)(2,1)S(1)}, u32[]{:S(2)}, u32[]{:S(2)}) collective-permute-start(bf16[128,256]{1,0:T(8,128)(2,1)S(1)} %get-tuple-element.31.kv0), channel_id=1, source_target_pairs={{0,8},{1,9},{2,10},{3,11},{4,12},{5,13},{6,14},{7,15},{8,0},{9,1},... | collective-permute-start | bytes 196616 | tf_op jit(solution)/shard_map/ppermute | solution.py:407
  15.6 1.2 %collective-permute-done.kv1 = bf16[128,256]{1,0:T(8,128)(2,1)S(1)} collective-permute-done((bf16[128,256]{1,0:T(8,128)(2,1)S(1)}, bf16[128,256]{1,0:T(8,128)(2,1)S(1)}, u32[]{:S(2)}, u32[]{:S(2)}) %collective-permute-start) | collective-permute-done | bytes 65568 | tf_op jit(solution)/shard_map/ppermute | solution.py:407
  16.8 2.4 %collective-permute-done.1.kv2 = bf16[128,256]{1,0:T(8,128)(2,1)S(1)} collective-permute-done((bf16[128,256]{1,0:T(8,128)(2,1)S(1)}, bf16[128,256]{1,0:T(8,128)(2,1)S(1)}, u32[]{:S(2)}, u32[]{:S(2)}) %collective-permute-start.1) | collective-permute-done | bytes 65568 | tf_op jit(solution)/shard_map/ppermute | solution.py:407
  19.2 0.0 collective-permute-done.2.qg1
  19.2 0.0 collective-permute-done.4.qg3
  19.2 2.2 %scores.1 = (f32[384,2048]{1,0:T(8,128)S(1)}, f32[384,2048]{1,0:T(8,128)S(1)}, f32[48,128]{1,0:T(8,128)S(1)}) custom-call(s32[1]{0:T(128)} %bitcast.where_ref, s32[1,8]{1,0:T(1,128)S(1)} %get-tuple-element.32.len_ref, bf16[128,256]{1,0:T(8,128)(2,1)S(1)} %get-tuple-element.31.kv0, bf16[128,256]{1,0:T(8,128)(2,1)S(1)} %collective-permute-done.kv1, ...), custom_call_target="tpu_custom_call" | custom-call | flops 400000000 | bytes 8000000 | tf_op jit(solution)/shard_map/scores/pallas_call | solution.py:218
  21.4 1.0 %collective-permute-start.5 = (f32[48,128]{1,0:T(8,128)S(1)}, f32[48,128]{1,0:T(8,128)S(1)}, u32[]{:S(2)}, u32[]{:S(2)}) collective-permute-start(f32[48,128]{1,0:T(8,128)S(1)} %get-tuple-element.36.st0), channel_id=1, source_target_pairs={{0,1},{1,0},{2,3},{3,2},{4,5},{5,4},{6,7},{7,6},{8,9},{9,8},{10,11... | collective-permute-start | bytes 73736 | tf_op jit(solution)/shard_map/ppermute | solution.py:407
  22.4 1.5 %collective-permute-start.6 = (f32[48,128]{1,0:T(8,128)S(1)}, f32[48,128]{1,0:T(8,128)S(1)}, u32[]{:S(2)}, u32[]{:S(2)}) collective-permute-start(f32[48,128]{1,0:T(8,128)S(1)} %get-tuple-element.36.st0), channel_id=1, source_target_pairs={{0,2},{1,3},{2,0},{3,1},{4,6},{5,7},{6,4},{7,5},{8,10},{9,11},{10,... | collective-permute-start | bytes 73736 | tf_op jit(solution)/shard_map/ppermute | solution.py:407
  23.8 0.3 collective-permute-start.7
  24.1 0.0 collective-permute-done.5.st1
  24.1 0.9 %collective-permute-done.6.st2 = f32[48,128]{1,0:T(8,128)S(1)} collective-permute-done((f32[48,128]{1,0:T(8,128)S(1)}, f32[48,128]{1,0:T(8,128)S(1)}, u32[]{:S(2)}, u32[]{:S(2)}) %collective-permute-start.6) | collective-permute-done | bytes 24608 | tf_op jit(solution)/shard_map/ppermute | solution.py:407
  25.0 2.0 %collective-permute-done.7.st3 = f32[48,128]{1,0:T(8,128)S(1)} collective-permute-done((f32[48,128]{1,0:T(8,128)S(1)}, f32[48,128]{1,0:T(8,128)S(1)}, u32[]{:S(2)}, u32[]{:S(2)}) %collective-permute-start.7) | collective-permute-done | bytes 24608 | tf_op jit(solution)/shard_map/ppermute | solution.py:407
  27.1 1.4 %gradients.1 = (f32[384,256]{1,0:T(8,128)S(1)}, bf16[384,256]{1,0:T(8,128)(2,1)S(1)}, f32[128,512]{1,0:T(8,128)S(1)}, bf16[128,512]{1,0:T(8,128)(2,1)S(1)}, bf16...) custom-call(bf16[128,256]{1,0:T(8,128)(2,1)S(1)} %get-tuple-element.31.kv0, ...), custom_call_target="tpu_custom_call" | custom-call | flops 600000000 | bytes 8000000 | tf_op jit(solution)/shard_map/gradients/pallas_call | solution.py:268
  28.4 1.7 %collective-permute-start.8 = (bf16[384,256]{1,0:T(8,128)(2,1)S(1)}, bf16[384,256]{1,0:T(8,128)(2,1)S(1)}, u32[]{:S(2)}, u32[]{:S(2)}) collective-permute-start(bf16[384,256]{1,0:T(8,128)(2,1)S(1)} %get-tuple-element.41), channel_id=1, source_target_pairs={{0,8},{1,9},{2,10},{3,11},{4,12},{5,13},{6,14},{7,15},{8,0},{9,1},... | collective-permute-start | bytes 589832 | tf_op jit(solution)/shard_map/ppermute | solution.py:407
  30.1 0.4 slices.1
  30.5 0.1 collective-permute-start.14
  30.6 2.3 %collective-permute-start.15 = (bf16[1024,128]{1,0:T(8,128)(2,1)S(1)}, bf16[1024,128]{1,0:T(8,128)(2,1)S(1)}, u32[]{:S(2)}, u32[]{:S(2)}) collective-permute-start(bf16[1024,128]{1,0:T(8,128)(2,1)S(1)} %get-tuple-element.50), channel_id=1, source_target_pairs={{0,8},{1,9},{2,10},{3,11},{4,12},{5,13},{6,14},{7,15},{8,0},{9,1},... | collective-permute-start | bytes 786440 | tf_op jit(solution)/shard_map/ppermute | solution.py:407
  32.9 1.1 %collective-permute-start.16 = (bf16[1024,128]{1,0:T(8,128)(2,1)S(1)}, bf16[1024,128]{1,0:T(8,128)(2,1)S(1)}, u32[]{:S(2)}, u32[]{:S(2)}) collective-permute-start(bf16[1024,128]{1,0:T(8,128)(2,1)S(1)} %get-tuple-element.51), channel_id=1, source_target_pairs={{0,12},{1,13},{2,14},{3,15},{4,0},{5,1},{6,2},{7,3},{8,4},{9,5},{1... | collective-permute-start | bytes 786440 | tf_op jit(solution)/shard_map/ppermute | solution.py:407
  34.0 0.4 collective-permute-start.12
  34.4 1.7 %collective-permute-done.8.r2 = bf16[384,256]{1,0:T(8,128)(2,1)S(1)} collective-permute-done((bf16[384,256]{1,0:T(8,128)(2,1)S(1)}, bf16[384,256]{1,0:T(8,128)(2,1)S(1)}, u32[]{:S(2)}, u32[]{:S(2)}) %collective-permute-start.8) | collective-permute-done | bytes 196640 | tf_op jit(solution)/shard_map/ppermute | solution.py:407
  36.1 0.6 collective-permute-start.13
  36.7 1.1 %tables.1.tab_ref = f32[512,256]{1,0:T(8,128)S(1)} custom-call(s32[1]{0:T(128)} %bitcast.where_ref), custom_call_target="tpu_custom_call" | custom-call | flops 2000000 | bytes 260000 | tf_op jit(solution)/shard_map/tables/pallas_call | solution.py:145
  37.8 5.4 %collective-permute-done.14.x1 = bf16[1024,128]{1,0:T(8,128)(2,1)S(1)} collective-permute-done((bf16[1024,128]{1,0:T(8,128)(2,1)S(1)}, bf16[1024,128]{1,0:T(8,128)(2,1)S(1)}, u32[]{:S(2)}, u32[]{:S(2)}) %collective-permute-start.14) | collective-permute-done | bytes 262176 | tf_op jit(solution)/shard_map/ppermute | solution.py:407
  43.2 4.2 %collective-permute-done.15.x2 = bf16[1024,128]{1,0:T(8,128)(2,1)S(1)} collective-permute-done((bf16[1024,128]{1,0:T(8,128)(2,1)S(1)}, bf16[1024,128]{1,0:T(8,128)(2,1)S(1)}, u32[]{:S(2)}, u32[]{:S(2)}) %collective-permute-start.15) | collective-permute-done | bytes 262176 | tf_op jit(solution)/shard_map/ppermute | solution.py:407
  47.4 0.0 collective-permute-done.16.x3
  47.4 4.9 %collective-permute-done.12.r1 = bf16[384,256]{1,0:T(8,128)(2,1)S(1)} collective-permute-done((bf16[384,256]{1,0:T(8,128)(2,1)S(1)}, bf16[384,256]{1,0:T(8,128)(2,1)S(1)}, u32[]{:S(2)}, u32[]{:S(2)}) %collective-permute-start.12) | collective-permute-done | bytes 196640 | tf_op jit(solution)/shard_map/ppermute | solution.py:407
  52.3 0.0 collective-permute-done.13.r3
  52.3 0.4 weight.1
  52.7 0.6 collective-permute-start.17
  53.3 0.3 own_half.1.own_ref
  53.6 0.9 %collective-permute-done.17.arrived_ref = bf16[512,256]{1,0:T(8,128)(2,1)S(1)} collective-permute-done((bf16[512,256]{1,0:T(8,128)(2,1)S(1)}, bf16[512,256]{1,0:T(8,128)(2,1)S(1)}, u32[]{:S(2)}, u32[]{:S(2)}) %collective-permute-start.17) | collective-permute-done | bytes 262176 | tf_op jit(solution)/shard_map/ppermute | solution.py:407
  54.5 0.7 weight_fold.1
  55.2 10.3 %all-to-all-start = ((bf16[32,16,256]{2,1,0:T(8,128)(2,1)}), bf16[32,16,256]{2,1,0:T(8,128)(2,1)S(1)}, u32[]{:S(2)}, u32[]{:S(2)}) async-start(bf16[32,16,256]{2,1,0:T(8,128)(2,1)} %bitcast.9), calls=%async_computation | async-start | bytes 524288 | tf_op jit(solution)/shard_map/all_to_all | solution.py:450
  65.6 1.3 %collective-permute-start.10 = (bf16[128,512]{1,0:T(8,128)(2,1)S(1)}, bf16[128,512]{1,0:T(8,128)(2,1)S(1)}, u32[]{:S(2)}, u32[]{:S(2)}) collective-permute-start(bf16[128,512]{1,0:T(8,128)(2,1)S(1)} %get-tuple-element.43), channel_id=1, source_target_pairs={{0,2},{1,3},{2,0},{3,1},{4,6},{5,7},{6,4},{7,5},{8,10},{9,11},{10,... | collective-permute-start | bytes 393224 | tf_op jit(solution)/shard_map/ppermute | solution.py:407
  66.9 1.1 %collective-permute-start.11 = (bf16[128,512]{1,0:T(8,128)(2,1)S(1)}, bf16[128,512]{1,0:T(8,128)(2,1)S(1)}, u32[]{:S(2)}, u32[]{:S(2)}) collective-permute-start(bf16[128,512]{1,0:T(8,128)(2,1)S(1)} %get-tuple-element.44), channel_id=1, source_target_pairs={{0,3},{1,2},{2,1},{3,0},{4,7},{5,6},{6,5},{7,4},{8,11},{9,10},{10,... | collective-permute-start | bytes 393224 | tf_op jit(solution)/shard_map/ppermute | solution.py:407
  67.9 0.2 collective-permute-start.9
  68.1 7.3 %collective-permute-done.10.r2 = bf16[128,512]{1,0:T(8,128)(2,1)S(1)} collective-permute-done((bf16[128,512]{1,0:T(8,128)(2,1)S(1)}, bf16[128,512]{1,0:T(8,128)(2,1)S(1)}, u32[]{:S(2)}, u32[]{:S(2)}) %collective-permute-start.10) | collective-permute-done | bytes 131104 | tf_op jit(solution)/shard_map/ppermute | solution.py:407
  75.4 4.0 %collective-permute-done.11.r3 = bf16[128,512]{1,0:T(8,128)(2,1)S(1)} collective-permute-done((bf16[128,512]{1,0:T(8,128)(2,1)S(1)}, bf16[128,512]{1,0:T(8,128)(2,1)S(1)}, u32[]{:S(2)}, u32[]{:S(2)}) %collective-permute-start.11) | collective-permute-done | bytes 131104 | tf_op jit(solution)/shard_map/ppermute | solution.py:407
  79.4 0.0 collective-permute-done.9.r1
  79.4 0.9 %query_end.1 = (bf16[128,512]{1,0:T(8,128)(2,1)}, bf16[128,128]{1,0:T(8,128)(2,1)}, bf16[128,128]{1,0:T(8,128)(2,1)}) custom-call(f32[128,512]{1,0:T(8,128)S(1)} %get-tuple-element.37.mine_ref, bf16[128,512]{1,0:T(8,128)(2,1)S(1)} %collective-permute-done.9.r1, bf16[128,512]{1,0:T(8,128)(2,1)S(1)} %collective-permute-done.10.r2, ...), custom_call_target="tpu_custom_call" | custom-call | flops 300000 | bytes 900000 | tf_op jit(solution)/shard_map/query_end/pallas_call | solution.py:299
  80.3 0.0 all-to-all-done
  80.3 0.7 convert_reduce_fusion
Async XLA Ops:
  2.1 7.5 %collective-permute-start.3 = (bf16[128,1024]{1,0:T(8,128)(2,1)S(1)}, bf16[128,1024]{1,0:T(8,128)(2,1)S(1)}, u32[]{:S(2)}, u32[]{:S(2)}) collective-permute-start(bf16[128,1024]{1,0:T(8,128)(2,1)S(1)} %get-tuple-element.33.qg0), channel_id=1, source_target_pairs={{0,2},{1,3},{2,0},{3,1},{4,6},{5,7},{6,4},{7,5},{8,10},{9,11},{10,... | collective-permute-start | bytes 786440 | tf_op jit(solution)/shard_map/ppermute | solution.py:407
  4.7 14.5 %collective-permute-start.2 = (bf16[128,1024]{1,0:T(8,128)(2,1)S(1)}, bf16[128,1024]{1,0:T(8,128)(2,1)S(1)}, u32[]{:S(2)}, u32[]{:S(2)}) collective-permute-start(bf16[128,1024]{1,0:T(8,128)(2,1)S(1)} %get-tuple-element.33.qg0), channel_id=1, source_target_pairs={{0,1},{1,0},{2,3},{3,2},{4,5},{5,4},{6,7},{7,6},{8,9},{9,8},{10,11... | collective-permute-start | bytes 786440 | tf_op jit(solution)/shard_map/ppermute | solution.py:407
  9.7 9.5 %collective-permute-start.4 = (bf16[128,1024]{1,0:T(8,128)(2,1)S(1)}, bf16[128,1024]{1,0:T(8,128)(2,1)S(1)}, u32[]{:S(2)}, u32[]{:S(2)}) collective-permute-start(bf16[128,1024]{1,0:T(8,128)(2,1)S(1)} %collective-permute-done.3.qg2), channel_id=1, source_target_pairs={{0,1},{1,0},{2,3},{3,2},{4,5},{5,4},{6,7},{7,6},{8,9},{9,8},{10,11... | collective-permute-start | bytes 786440 | tf_op jit(solution)/shard_map/ppermute | solution.py:407
  11.9 4.9 %collective-permute-start = (bf16[128,256]{1,0:T(8,128)(2,1)S(1)}, bf16[128,256]{1,0:T(8,128)(2,1)S(1)}, u32[]{:S(2)}, u32[]{:S(2)}) collective-permute-start(bf16[128,256]{1,0:T(8,128)(2,1)S(1)} %get-tuple-element.31.kv0), channel_id=1, source_target_pairs={{0,4},{1,5},{2,6},{3,7},{4,8},{5,9},{6,10},{7,11},{8,12},{9,13},{1... | collective-permute-start | bytes 196616 | tf_op jit(solution)/shard_map/ppermute | solution.py:407
  13.1 6.0 %collective-permute-start.1 = (bf16[128,256]{1,0:T(8,128)(2,1)S(1)}, bf16[128,256]{1,0:T(8,128)(2,1)S(1)}, u32[]{:S(2)}, u32[]{:S(2)}) collective-permute-start(bf16[128,256]{1,0:T(8,128)(2,1)S(1)} %get-tuple-element.31.kv0), channel_id=1, source_target_pairs={{0,8},{1,9},{2,10},{3,11},{4,12},{5,13},{6,14},{7,15},{8,0},{9,1},... | collective-permute-start | bytes 196616 | tf_op jit(solution)/shard_map/ppermute | solution.py:407
  21.4 2.7 %collective-permute-start.5 = (f32[48,128]{1,0:T(8,128)S(1)}, f32[48,128]{1,0:T(8,128)S(1)}, u32[]{:S(2)}, u32[]{:S(2)}) collective-permute-start(f32[48,128]{1,0:T(8,128)S(1)} %get-tuple-element.36.st0), channel_id=1, source_target_pairs={{0,1},{1,0},{2,3},{3,2},{4,5},{5,4},{6,7},{7,6},{8,9},{9,8},{10,11... | collective-permute-start | bytes 73736 | tf_op jit(solution)/shard_map/ppermute | solution.py:407
  22.4 2.7 %collective-permute-start.6 = (f32[48,128]{1,0:T(8,128)S(1)}, f32[48,128]{1,0:T(8,128)S(1)}, u32[]{:S(2)}, u32[]{:S(2)}) collective-permute-start(f32[48,128]{1,0:T(8,128)S(1)} %get-tuple-element.36.st0), channel_id=1, source_target_pairs={{0,2},{1,3},{2,0},{3,1},{4,6},{5,7},{6,4},{7,5},{8,10},{9,11},{10,... | collective-permute-start | bytes 73736 | tf_op jit(solution)/shard_map/ppermute | solution.py:407
  23.8 3.3 %collective-permute-start.7 = (f32[48,128]{1,0:T(8,128)S(1)}, f32[48,128]{1,0:T(8,128)S(1)}, u32[]{:S(2)}, u32[]{:S(2)}) collective-permute-start(f32[48,128]{1,0:T(8,128)S(1)} %get-tuple-element.36.st0), channel_id=1, source_target_pairs={{0,3},{1,2},{2,1},{3,0},{4,7},{5,6},{6,5},{7,4},{8,11},{9,10},{10,... | collective-permute-start | bytes 73736 | tf_op jit(solution)/shard_map/ppermute | solution.py:407
  28.4 7.7 %collective-permute-start.8 = (bf16[384,256]{1,0:T(8,128)(2,1)S(1)}, bf16[384,256]{1,0:T(8,128)(2,1)S(1)}, u32[]{:S(2)}, u32[]{:S(2)}) collective-permute-start(bf16[384,256]{1,0:T(8,128)(2,1)S(1)} %get-tuple-element.41), channel_id=1, source_target_pairs={{0,8},{1,9},{2,10},{3,11},{4,12},{5,13},{6,14},{7,15},{8,0},{9,1},... | collective-permute-start | bytes 589832 | tf_op jit(solution)/shard_map/ppermute | solution.py:407
  30.5 12.7 %collective-permute-start.14 = (bf16[1024,128]{1,0:T(8,128)(2,1)S(1)}, bf16[1024,128]{1,0:T(8,128)(2,1)S(1)}, u32[]{:S(2)}, u32[]{:S(2)}) collective-permute-start(bf16[1024,128]{1,0:T(8,128)(2,1)S(1)} %get-tuple-element.49), channel_id=1, source_target_pairs={{0,4},{1,5},{2,6},{3,7},{4,8},{5,9},{6,10},{7,11},{8,12},{9,13},{1... | collective-permute-start | bytes 786440 | tf_op jit(solution)/shard_map/ppermute | solution.py:407
  30.6 16.8 %collective-permute-start.15 = (bf16[1024,128]{1,0:T(8,128)(2,1)S(1)}, bf16[1024,128]{1,0:T(8,128)(2,1)S(1)}, u32[]{:S(2)}, u32[]{:S(2)}) collective-permute-start(bf16[1024,128]{1,0:T(8,128)(2,1)S(1)} %get-tuple-element.50), channel_id=1, source_target_pairs={{0,8},{1,9},{2,10},{3,11},{4,12},{5,13},{6,14},{7,15},{8,0},{9,1},... | collective-permute-start | bytes 786440 | tf_op jit(solution)/shard_map/ppermute | solution.py:407
  32.9 14.5 %collective-permute-start.16 = (bf16[1024,128]{1,0:T(8,128)(2,1)S(1)}, bf16[1024,128]{1,0:T(8,128)(2,1)S(1)}, u32[]{:S(2)}, u32[]{:S(2)}) collective-permute-start(bf16[1024,128]{1,0:T(8,128)(2,1)S(1)} %get-tuple-element.51), channel_id=1, source_target_pairs={{0,12},{1,13},{2,14},{3,15},{4,0},{5,1},{6,2},{7,3},{8,4},{9,5},{1... | collective-permute-start | bytes 786440 | tf_op jit(solution)/shard_map/ppermute | solution.py:407
  34.0 18.3 %collective-permute-start.12 = (bf16[384,256]{1,0:T(8,128)(2,1)S(1)}, bf16[384,256]{1,0:T(8,128)(2,1)S(1)}, u32[]{:S(2)}, u32[]{:S(2)}) collective-permute-start(bf16[384,256]{1,0:T(8,128)(2,1)S(1)} %get-tuple-element.41), channel_id=1, source_target_pairs={{0,4},{1,5},{2,6},{3,7},{4,8},{5,9},{6,10},{7,11},{8,12},{9,13},{1... | collective-permute-start | bytes 589832 | tf_op jit(solution)/shard_map/ppermute | solution.py:407
  36.1 16.2 %collective-permute-start.13 = (bf16[384,256]{1,0:T(8,128)(2,1)S(1)}, bf16[384,256]{1,0:T(8,128)(2,1)S(1)}, u32[]{:S(2)}, u32[]{:S(2)}) collective-permute-start(bf16[384,256]{1,0:T(8,128)(2,1)S(1)} %get-tuple-element.41), channel_id=1, source_target_pairs={{0,12},{1,13},{2,14},{3,15},{4,0},{5,1},{6,2},{7,3},{8,4},{9,5},{1... | collective-permute-start | bytes 589832 | tf_op jit(solution)/shard_map/ppermute | solution.py:407
  52.7 1.7 %collective-permute-start.17 = (bf16[512,256]{1,0:T(8,128)(2,1)S(1)}, bf16[512,256]{1,0:T(8,128)(2,1)S(1)}, u32[]{:S(2)}, u32[]{:S(2)}) collective-permute-start(bf16[512,256]{1,0:T(8,128)(2,1)S(1)} %get-tuple-element.57), channel_id=1, source_target_pairs={{0,1},{1,0},{2,3},{3,2},{4,5},{5,4},{6,7},{7,6},{8,9},{9,8},{10,11... | collective-permute-start | bytes 786440 | tf_op jit(solution)/shard_map/ppermute | solution.py:407
  55.2 25.1 %all-to-all-start = ((bf16[32,16,256]{2,1,0:T(8,128)(2,1)}), bf16[32,16,256]{2,1,0:T(8,128)(2,1)S(1)}, u32[]{:S(2)}, u32[]{:S(2)}) async-start(bf16[32,16,256]{2,1,0:T(8,128)(2,1)} %bitcast.9), calls=%async_computation | async-start | bytes 524288 | tf_op jit(solution)/shard_map/all_to_all | solution.py:450
  65.6 9.8 %collective-permute-start.10 = (bf16[128,512]{1,0:T(8,128)(2,1)S(1)}, bf16[128,512]{1,0:T(8,128)(2,1)S(1)}, u32[]{:S(2)}, u32[]{:S(2)}) collective-permute-start(bf16[128,512]{1,0:T(8,128)(2,1)S(1)} %get-tuple-element.43), channel_id=1, source_target_pairs={{0,2},{1,3},{2,0},{3,1},{4,6},{5,7},{6,4},{7,5},{8,10},{9,11},{10,... | collective-permute-start | bytes 393224 | tf_op jit(solution)/shard_map/ppermute | solution.py:407
  66.9 12.5 %collective-permute-start.11 = (bf16[128,512]{1,0:T(8,128)(2,1)S(1)}, bf16[128,512]{1,0:T(8,128)(2,1)S(1)}, u32[]{:S(2)}, u32[]{:S(2)}) collective-permute-start(bf16[128,512]{1,0:T(8,128)(2,1)S(1)} %get-tuple-element.44), channel_id=1, source_target_pairs={{0,3},{1,2},{2,1},{3,0},{4,7},{5,6},{6,5},{7,4},{8,11},{9,10},{10,... | collective-permute-start | bytes 393224 | tf_op jit(solution)/shard_map/ppermute | solution.py:407
  67.9 11.4 %collective-permute-start.9 = (bf16[128,512]{1,0:T(8,128)(2,1)S(1)}, bf16[128,512]{1,0:T(8,128)(2,1)S(1)}, u32[]{:S(2)}, u32[]{:S(2)}) collective-permute-start(bf16[128,512]{1,0:T(8,128)(2,1)S(1)} %get-tuple-element.42), channel_id=1, source_target_pairs={{0,1},{1,0},{2,3},{3,2},{4,5},{5,4},{6,7},{7,6},{8,9},{9,8},{10,11... | collective-permute-start | bytes 393224 | tf_op jit(solution)/shard_map/ppermute | solution.py:407
